TPU v7x, 32 devices: a whole 2x2x4 slice. The times are simulated.
32 devices in a mesh: rows: 8 (over z, x), cols: 4 (over y, core).
Axes of the slice: x: 2, y: 2, z: 4, core: 2. Of those that a mesh axis runs over, the one named last changes fastest.
Arguments:
- row_features: float32 [4096, 64], P('rows'), may hold values from -6 to 6, as said below
- col_features: float32 [16384, 64], P('cols'), may hold values from -6 to 6, as said below
- test_block: bfloat16 [16384, 256], P('cols'), may hold values from -0.046875 to 0.046875, as said below
Outputs:
- basis: float32 [4096, 256], P('rows', 'cols')
- projected: float32 [256, 16384], P('rows', 'cols')
Inputs may be any that keep to these rules, and one draw needn't show every extreme that they name: `row_features`: independent entries of mean zero and unit variance. `col_features`: independent entries of mean zero and unit variance. `test_block`: independent entries of mean zero and variance 1 / 16384.
All inputs are finite; a program needn't handle non-finite values.
Results may differ from a plain program's by a relative error of at most 0.0095.
Values may be sent and summed in bfloat16 or wider, within the bound.
No kernel may reach another device: no remote copies, remote signals or barrier semaphores. Data moves between devices by JAX's collectives and lax.ppermute only.
A program may use at most 64 MiB of HBM per device.

v0:
```python
import math
import jax
import jax.numpy as jnp
from jax import lax
from jax.sharding import PartitionSpec as P


def kernel_tile(rows, cols):
    width = rows.shape[1]
    inner = lax.dot_general(
        rows,
        cols,
        (((1,), (1,)), ((), ())),
        precision=lax.Precision.HIGHEST,
        preferred_element_type=jnp.float32,
    ) * (1.0 / math.sqrt(width))
    shifted = inner + 1.0
    return (shifted * shifted * shifted).astype(jnp.bfloat16)


def gram_of(values):
    return lax.dot_general(
        values,
        values,
        (((0,), (0,)), ((), ())),
        precision=lax.Precision.HIGHEST,
        preferred_element_type=jnp.float32,
    )


def local(row_features, col_features, test_block):
    tile = kernel_tile(row_features, col_features)
    partial_sketch = jnp.dot(tile, test_block, preferred_element_type=jnp.float32)
    columns = partial_sketch.shape[1]
    own_width = columns // lax.axis_size("cols")
    sketch = lax.psum(partial_sketch, "cols")
    gram = lax.psum(gram_of(sketch), "rows")
    lower = jnp.linalg.cholesky(gram)
    basis_full = jax.scipy.linalg.solve_triangular(lower, sketch.T, lower=True).T
    basis = lax.dynamic_slice_in_dim(basis_full, lax.axis_index("cols") * own_width, own_width, 1)
    basis_b = basis_full.astype(jnp.bfloat16)
    projected = lax.psum_scatter(
        lax.dot_general(
            basis_b, tile, (((0,), (0,)), ((), ())), preferred_element_type=jnp.float32
        ).astype(jnp.bfloat16),
        "rows",
        scatter_dimension=0,
        tiled=True,
    ).astype(jnp.float32)
    return (basis, projected)


def solution(mesh):
    in_specs = (P("rows", None), P("cols", None), P("cols", None))
    out_specs = (P("rows", "cols"), P("rows", "cols"))
    return jax.shard_map(local, mesh=mesh, in_specs=in_specs, out_specs=out_specs, check_vma=False)
```

profile of v0, /device:TPU:0, one launch (start us, length us, event | category | flops | bytes accessed | tf_op | source)
XLA Modules:
  0.0 276.0 jit_solution(16074343065855323033)
XLA Ops:
  7.2 0.0 copy-start
  7.2 0.0 all-reduce.4.cloned.1.call-start
  7.2 9.1 %fusion = bf16[512,4096]{1,0:T(8,128)(2,1)S(1)} fusion(f32[512,64]{0,1:T(8,128)} %param.3, f32[4096,64]{0,1:T(8,128)} %param.4), kind=kOutput, calls=%fused_computation.3 | convolution fusion | flops 1621098496 | bytes 5373952 | tf_op jit(solution)/shard_map/dot_general | solution.py:10
  16.3 0.0 copy-start.2
  16.3 1.9 copy-done.2
  18.3 0.0 copy-done
  18.3 2.1 fusion.15
  20.3 0.0 all-reduce.4.cloned.1.call-update
  20.4 0.0 all-reduce.6.cloned.1.call-start
  20.4 36.3 %all-reduce.4.cloned.1.call-done = f32[512,256]{1,0:T(8,128)} async-done(((f32[512,256]{1,0:T(8,128)}), f32[512,256]{1,0:T(8,128)}) %all-reduce.4.cloned.1.call-update) | async-done | bytes 524304 | tf_op jit(solution)/shard_map/psum | solution.py:36
  56.7 0.0 copy-start.1
  56.7 3.0 %fusion.16 = f32[256,256]{0,1:T(8,128)} fusion(f32[512,256]{1,0:T(8,128)} %all-reduce.4.cloned.1.call-done), kind=kOutput, calls=%fused_computation.39 | convolution fusion | flops 402653184 | bytes 786432 | tf_op jit(solution)/shard_map/dot_general | solution.py:22
  59.6 0.0 all-reduce.6.cloned.1.call-update
  59.7 0.2 reduce-scatter.2.cloned.1.call-start
  59.9 71.9 %all-reduce.6.cloned.1.call-done = f32[256,256]{0,1:T(8,128)} async-done(((f32[256,256]{0,1:T(8,128)}), f32[256,256]{0,1:T(8,128)}) %all-reduce.6.cloned.1.call-update) | async-done | bytes 262160 | tf_op jit(solution)/shard_map/psum | solution.py:37
  131.8 1.1 copy.6
  132.9 1.0 fusion.5
  133.9 11.7 %cholesky.50 = f32[128,128]{1,0:T(8,128)S(1)} custom-call(f32[128,128]{1,0:T(8,128)S(1)} %cholesky.118), custom_call_target="Cholesky" | custom-call | tf_op jit(solution)/shard_map/jit(cholesky)/cholesky | solution.py:38
  145.6 9.8 %custom-call.15 = f32[1,128,128]{1,2,0:T(8,128)S(1)} custom-call(f32[1,128,128]{2,1,0:T(8,128)S(1)} %get-tuple-element.23), custom_call_target="InvertDiagBlocksLowerTriangular" | custom-call | tf_op jit(solution)/shard_map/jit(cholesky)/cholesky | solution.py:38
  155.5 0.2 constant_dynamic-update-slice_fusion
  155.7 0.3 convolution_subtract_fusion.1
  155.9 11.7 %cholesky.105 = f32[128,128]{1,0:T(8,128)S(1)} custom-call(f32[128,128]{1,0:T(8,128)S(1)} %convolution_subtract_fusion.1), custom_call_target="Cholesky" | custom-call | tf_op jit(solution)/shard_map/jit(cholesky)/cholesky | solution.py:38
  167.7 0.6 compare_reduce_fusion
  169.6 0.1 triangular_solve.57
  169.7 4.0 %while.1 = (s32[]{:T(128)}, f32[256,256]{1,0:T(8,128)S(1)}, s32[2,2]{1,0:T(2,128)S(1)}, f32[2,128,128]{2,1,0:T(8,128)S(1)}, s32[]{:T(128)}) while((s32[]{:T(128)}, f32[256,256]{1,0:T(8,128)S(1)}, s32[2,2]{1,0:T(2,128)S(1)}, f32[2,128,128]{2,1,0:T(8,128)S(1)}, s32[]{:T(128)}) %tuple.27), condition=%wide.while_cond, body=%wide.while_body.sunk | while | flops 2 | bytes 131181 | solution.py:39
  169.8 0.6 fusion.29
  170.4 1.3 bitcast_dynamic-update-slice_fusion.2
  171.7 0.6 fusion.29
  172.3 1.3 bitcast_dynamic-update-slice_fusion.2
  173.6 19.7 %custom-call.16 = f32[2,128,128]{1,2,0:T(8,128)S(1)} custom-call(f32[2,128,128]{2,1,0:T(8,128)S(1)} %get-tuple-element.9), custom_call_target="InvertDiagBlocksLowerTriangular" | custom-call | tf_op jit(solution)/shard_map/jit(_solve_triangular)/triangular_solve | solution.py:39
  193.3 0.0 copy-done.1
  193.3 0.4 fusion.3
  193.7 0.6 convolution_subtract_fusion
  194.3 0.4 fusion.9
  194.8 4.8 %convolution_convert_fusion = bf16[256,4096]{1,0:T(8,128)(2,1)} fusion(bf16[512,4096]{1,0:T(8,128)(2,1)} %copy-done.2, f32[128,512]{1,0:T(8,128)S(1)} %fusion.9, f32[128,512]{1,0:T(8,128)S(1)} %fusion.3), kind=kOutput, calls=%fused_computation.4 | convolution fusion | flops 1075314688 | bytes 6815744 | tf_op jit(solution)/shard_map/dot_general | solution.py:43
  199.5 0.0 reduce-scatter.2.cloned.1.call-update
  199.6 0.7 fusion.7
  200.3 67.4 %reduce-scatter.2.cloned.1.call-done = bf16[32,4096]{1,0:T(8,128)(2,1)} async-done(((bf16[256,4096]{1,0:T(8,128)(2,1)}), bf16[32,4096]{1,0:T(8,128)(2,1)}) %reduce-scatter.2.cloned.1.call-update) | async-done | bytes 262160 | tf_op jit(solution)/shard_map/reduce_scatter | solution.py:42
  267.7 1.8 convert_element_type.16
  (9 shorter events, 0.1 us)
Async XLA Ops:
  7.2 11.1 %copy-start = (bf16[4096,256]{1,0:T(8,128)(2,1)S(1)}, bf16[4096,256]{1,0:T(8,128)(2,1)}, u32[]{:S(2)}) copy-start(bf16[4096,256]{1,0:T(8,128)(2,1)} %param.5) | copy-start | bytes 6291460
  7.2 49.5 %all-reduce.4.cloned.1.call-start = ((), (), s32[]{:S(2)}) async-start(), calls=%async_computation.1 | async-start | bytes 1048576 | tf_op jit(solution)/shard_map/psum | solution.py:36
  16.3 1.9 copy-start.2
  20.4 111.4 %all-reduce.6.cloned.1.call-start = ((), (), s32[]{:S(2)}) async-start(), calls=%async_computation.2 | async-start | bytes 524288 | tf_op jit(solution)/shard_map/psum | solution.py:37
  56.7 136.6 %copy-start.1 = (f32[512,256]{1,0:T(8,128)S(1)}, f32[512,256]{1,0:T(8,128)}, u32[]{:S(2)}) copy-start(f32[512,256]{1,0:T(8,128)} %all-reduce.4.cloned.1.call-done) | copy-start | bytes 1572868
  59.7 208.0 %reduce-scatter.2.cloned.1.call-start = ((), (), s32[]{:S(2)}) async-start(), calls=%async_computation.3 | async-start | bytes 2359296 | tf_op jit(solution)/shard_map/reduce_scatter | solution.py:42
Sparse Core Ops, SparseCore 0:
  20.5 36.1 all-reduce.3
  60.6 71.1 all-reduce.5
  199.7 67.9 reduce-scatter.1
where the time goes:
time: 276 us
  waiting for transfers between devices  176 us (64%)
  other arithmetic  57.1 us (21%)
  matrix products  20.8 us (8%)
  between operations  15.1 us (5%)
  local copies, waits for them, and re-layouts  6.85 us (2%)
    psum x1, waiting for transfers between devices, local(): gram = lax.psum(gram_of(sketch), 'rows')  71.9 us
    reduce_scatter x1, waiting for transfers between devices, local(): lax.psum_scatter(lax.dot_general(basis_b, tile, (((0,), (0,)), ((), ())),...  67.4 us
    psum x1, waiting for transfers between devices, local(): sketch = lax.psum(partial_sketch, 'cols')  36.3 us
    another operation x6, other arithmetic, local(): lower = jnp.linalg.cholesky(gram)  34 us
    another operation x3, other arithmetic, local(): jax.scipy.linalg.solve_triangular(lower, sketch.T, lower=True)  19.7 us
    dot_general x1, matrix products, kernel_tile(): lax.dot_general(rows, cols, (((1,), (1,)), ((), ())), precision=lax.Preci...  9.1 us
  transfers between devices with their start and end apart: 3, of which 3 were waited for; matrix products, arithmetic and copies ran while one was open for 0% of the time, Pallas kernels for 0%

commit v1 on v0

--- a/solution.py
+++ b/solution.py
@@ -34,7 +34,9 @@
     columns = partial_sketch.shape[1]
     own_width = columns // lax.axis_size("cols")
     sketch = lax.psum(partial_sketch, "cols")
-    gram = lax.psum(gram_of(sketch), "rows")
+    block = gram_of(sketch)
+    blocks = lax.all_gather(block, "rows", axis=0, tiled=False)
+    gram = blocks.sum(axis=0)
     lower = jnp.linalg.cholesky(gram)
     basis_full = jax.scipy.linalg.solve_triangular(lower, sketch.T, lower=True).T
     basis = lax.dynamic_slice_in_dim(basis_full, lax.axis_index("cols") * own_width, own_width, 1)

time: 276 us -> 253 us (0.917)
  waiting for transfers between devices: 176 us -> 152 us
    psum x1 -> x0, waiting for transfers between devices: 71.9 us -> none  [local(): gram = lax.psum(gram_of(sketch), 'rows')]
    all_gather x0 -> x1, waiting for transfers between devices: none -> 49.1 us  [local(): blocks = lax.all_gather(block, 'rows', axis=0, tiled=False)]
where the time goes in v1:
time: 253 us
  waiting for transfers between devices  152 us (60%)
  other arithmetic  57.9 us (23%)
  matrix products  20.8 us (8%)
  between operations  15.2 us (6%)
  local copies, waits for them, and re-layouts  6.05 us (2%)
    reduce_scatter x1, waiting for transfers between devices, local(): lax.psum_scatter(lax.dot_general(basis_b, tile, (((0,), (0,)), ((), ())),...  66.8 us
    all_gather x1, waiting for transfers between devices, local(): blocks = lax.all_gather(block, 'rows', axis=0, tiled=False)  49.1 us
    psum x1, waiting for transfers between devices, local(): sketch = lax.psum(partial_sketch, 'cols')  36.3 us
    another operation x6, other arithmetic, local(): lower = jnp.linalg.cholesky(gram)  34 us
    another operation x3, other arithmetic, local(): jax.scipy.linalg.solve_triangular(lower, sketch.T, lower=True)  19.7 us
    dot_general x1, matrix products, kernel_tile(): lax.dot_general(rows, cols, (((1,), (1,)), ((), ())), precision=lax.Preci...  9.1 us
  transfers between devices with their start and end apart: 3, of which 3 were waited for; matrix products, arithmetic and copies ran while one was open for 0% of the time, Pallas kernels for 0%

profile of v1, /device:TPU:0, one launch (start us, length us, event | category | flops | bytes accessed | tf_op | source)
XLA Modules:
  0.0 252.7 jit_solution(18008934259691905412)
XLA Ops:
  7.2 0.0 copy-start
  7.2 0.0 all-reduce.3.cloned.1.call-start
  7.2 9.1 %fusion = bf16[512,4096]{1,0:T(8,128)(2,1)S(1)} fusion(f32[512,64]{0,1:T(8,128)} %param.3, f32[4096,64]{0,1:T(8,128)} %param.4), kind=kOutput, calls=%fused_computation.3 | convolution fusion | flops 1621098496 | bytes 5373952 | tf_op jit(solution)/shard_map/dot_general | solution.py:10
  16.3 0.0 copy-start.2
  16.3 1.9 copy-done.2
  18.3 0.0 copy-done
  18.3 2.1 fusion.15
  20.3 0.0 all-reduce.3.cloned.1.call-update
  20.4 0.0 all-gather.3.cloned.1.call-start
  20.4 36.3 %all-reduce.3.cloned.1.call-done = f32[512,256]{1,0:T(8,128)} async-done(((f32[512,256]{1,0:T(8,128)}), f32[512,256]{1,0:T(8,128)}) %all-reduce.3.cloned.1.call-update) | async-done | bytes 524304 | tf_op jit(solution)/shard_map/psum | solution.py:36
  56.7 0.0 copy-start.1
  56.7 3.0 %fusion.16 = f32[256,256]{1,0:T(8,128)} fusion(f32[512,256]{1,0:T(8,128)} %all-reduce.3.cloned.1.call-done), kind=kOutput, calls=%fused_computation.39 | convolution fusion | flops 402653184 | bytes 786432 | tf_op jit(solution)/shard_map/dot_general | solution.py:22
  59.7 0.0 all-gather.3.cloned.1.call-update
  59.7 0.2 reduce-scatter.2.cloned.1.call-start
  59.9 49.1 %all-gather.3.cloned.1.call-done = f32[2048,256]{1,0:T(8,128)} async-done(((f32[256,256]{1,0:T(8,128)}), f32[2048,256]{1,0:T(8,128)}) %all-gather.3.cloned.1.call-update) | async-done | bytes 2097168 | tf_op jit(solution)/shard_map/all_gather | solution.py:38
  109.0 1.8 reduce_sum.9
  110.8 0.1 copy.6
  111.0 11.7 %cholesky.50 = f32[128,128]{1,0:T(8,128)S(1)} custom-call(f32[128,128]{1,0:T(8,128)S(1)} %cholesky.118), custom_call_target="Cholesky" | custom-call | tf_op jit(solution)/shard_map/jit(cholesky)/cholesky | solution.py:40
  122.7 9.8 %custom-call.15 = f32[1,128,128]{1,2,0:T(8,128)S(1)} custom-call(f32[1,128,128]{2,1,0:T(8,128)S(1)} %get-tuple-element.23), custom_call_target="InvertDiagBlocksLowerTriangular" | custom-call | tf_op jit(solution)/shard_map/jit(cholesky)/cholesky | solution.py:40
  132.6 0.2 constant_dynamic-update-slice_fusion
  132.8 0.3 convolution_subtract_fusion.1
  133.0 11.7 %cholesky.105 = f32[128,128]{1,0:T(8,128)S(1)} custom-call(f32[128,128]{1,0:T(8,128)S(1)} %convolution_subtract_fusion.1), custom_call_target="Cholesky" | custom-call | tf_op jit(solution)/shard_map/jit(cholesky)/cholesky | solution.py:40
  144.8 0.7 compare_reduce_fusion
  146.8 0.1 triangular_solve.57
  146.8 4.1 %while.1 = (s32[]{:T(128)}, f32[256,256]{1,0:T(8,128)S(1)}, s32[2,2]{1,0:T(2,128)S(1)}, f32[2,128,128]{2,1,0:T(8,128)S(1)}, s32[]{:T(128)}) while((s32[]{:T(128)}, f32[256,256]{1,0:T(8,128)S(1)}, s32[2,2]{1,0:T(2,128)S(1)}, f32[2,128,128]{2,1,0:T(8,128)S(1)}, s32[]{:T(128)}) %tuple.27), condition=%wide.while_cond, body=%wide.while_body.sunk | while | flops 2 | bytes 131181 | solution.py:41
  147.0 0.6 fusion.29
  147.6 1.4 bitcast_dynamic-update-slice_fusion.2
  149.0 0.6 fusion.29
  149.6 1.4 bitcast_dynamic-update-slice_fusion.2
  150.9 19.7 %custom-call.16 = f32[2,128,128]{1,2,0:T(8,128)S(1)} custom-call(f32[2,128,128]{2,1,0:T(8,128)S(1)} %get-tuple-element.9), custom_call_target="InvertDiagBlocksLowerTriangular" | custom-call | tf_op jit(solution)/shard_map/jit(_solve_triangular)/triangular_solve | solution.py:41
  170.6 0.0 copy-done.1
  170.6 0.4 fusion.3
  171.1 0.6 convolution_subtract_fusion
  171.7 0.4 fusion.9
  172.1 4.8 %convolution_convert_fusion = bf16[256,4096]{1,0:T(8,128)(2,1)} fusion(bf16[512,4096]{1,0:T(8,128)(2,1)} %copy-done.2, f32[128,512]{1,0:T(8,128)S(1)} %fusion.9, f32[128,512]{1,0:T(8,128)S(1)} %fusion.3), kind=kOutput, calls=%fused_computation.4 | convolution fusion | flops 1075314688 | bytes 6815744 | tf_op jit(solution)/shard_map/dot_general | solution.py:45
  176.9 0.0 reduce-scatter.2.cloned.1.call-update
  176.9 0.7 fusion.7
  177.6 66.8 %reduce-scatter.2.cloned.1.call-done = bf16[32,4096]{1,0:T(8,128)(2,1)} async-done(((bf16[256,4096]{1,0:T(8,128)(2,1)}), bf16[32,4096]{1,0:T(8,128)(2,1)}) %reduce-scatter.2.cloned.1.call-update) | async-done | bytes 262160 | tf_op jit(solution)/shard_map/reduce_scatter | solution.py:44
  244.4 1.8 convert_element_type.16
  (10 shorter events, 0.2 us)
Async XLA Ops:
  7.2 11.1 %copy-start = (bf16[4096,256]{1,0:T(8,128)(2,1)S(1)}, bf16[4096,256]{1,0:T(8,128)(2,1)}, u32[]{:S(2)}) copy-start(bf16[4096,256]{1,0:T(8,128)(2,1)} %param.5) | copy-start | bytes 6291460
  7.2 49.5 %all-reduce.3.cloned.1.call-start = ((), (), s32[]{:S(2)}) async-start(), calls=%async_computation.1 | async-start | bytes 1048576 | tf_op jit(solution)/shard_map/psum | solution.py:36
  16.3 1.9 copy-start.2
  20.4 88.6 %all-gather.3.cloned.1.call-start = ((), (), s32[]{:S(2)}) async-start(), calls=%async_computation.3 | async-start | bytes 2359296 | tf_op jit(solution)/shard_map/all_gather | solution.py:38
  56.7 113.9 %copy-start.1 = (f32[512,256]{1,0:T(8,128)S(1)}, f32[512,256]{1,0:T(8,128)}, u32[]{:S(2)}) copy-start(f32[512,256]{1,0:T(8,128)} %all-reduce.3.cloned.1.call-done) | copy-start | bytes 1572868
  59.7 184.7 %reduce-scatter.2.cloned.1.call-start = ((), (), s32[]{:S(2)}) async-start(), calls=%async_computation.2 | async-start | bytes 2359296 | tf_op jit(solution)/shard_map/reduce_scatter | solution.py:44
Sparse Core Ops, SparseCore 0:
  20.5 36.1 all-reduce.2
  59.8 49.1 all-gather.2
  177.0 67.3 reduce-scatter.1
